TPU v7x, 32 devices: a whole 2x2x4 slice. The times are simulated.
32 devices in a mesh: site: 16 (over z, x, core), fsdp: 2 (over y).
Axes of the slice: x: 2, y: 2, z: 4, core: 2. Of those that a mesh axis runs over, the one named last changes fastest.
Arguments:
- tokens: bfloat16 [4096, 5120], P(('site', 'fsdp')), may hold values from -6 to 6
- norm_gain: float32 [5120], replicated, may hold values from 0.1 to 1.9
- state: bfloat16 [16, 5120, 1024], P('site', 'fsdp'), may hold values from -6 to 6
- weight_sum: float32 [16], P('site'), may hold values from 0.5 to 2
- key_value_grad: bfloat16 [4096, 1024], P(('site', 'fsdp')), may hold values from -6 to 6
- round_number: int32 [1], replicated, may hold values from 0 to 1048575
Outputs:
- projected: bfloat16 [4096, 1024], P(('site', 'fsdp'))
- new_state: bfloat16 [16, 5120, 1024], P('site', 'fsdp')
- new_weight: float32 [16], P('site')
Inputs may be any that keep to these rules, and one draw needn't show every extreme that they name: With k = round_number mod 4, site s pushes to site (s + 2^k) mod 16.
All inputs are finite; a program needn't handle non-finite values.
Results may differ from a plain program's by a relative error of at most 0.0058.
Values may be sent and summed in bfloat16 or wider, within the bound.
A program may use at most 128 MiB of HBM per device.

v0:
```python
from functools import partial

import jax
import jax.numpy as jnp
from jax import lax
from jax.sharding import PartitionSpec as P

KMAX = 4


def shifted(block, axis, distance):
    devices = range(lax.axis_size(axis))
    route = [((i - distance) % len(devices), i) for i in devices]
    return lax.ppermute(block, axis, route)


def rms_normed(tokens, norm_gain):
    values = tokens.astype(jnp.float32)
    inverse = lax.rsqrt(jnp.mean(values * values, axis=1, keepdims=True) + 1e-06)
    return (values * inverse * norm_gain).astype(jnp.bfloat16)


def push_updated(payload, offset):
    return shifted((payload[0], payload[1]), "site", offset)


def along_loop(sender, payload, round_number):
    branches = [partial(sender, offset=2**exponent) for exponent in range(KMAX)]
    which = jnp.remainder(round_number[0], jnp.int32(KMAX))
    return lax.switch(which, branches, payload)


def body(tokens, norm_gain, state, weight_sum, key_value_grad, round_number):
    factor = tokens.shape[1] ** (-0.5)
    normed = rms_normed(tokens, norm_gain)
    stored = state[0]
    debiased = (stored.astype(jnp.float32) / weight_sum[0]).astype(jnp.bfloat16)
    columns = lax.all_to_all(normed, "fsdp", split_axis=1, concat_axis=0, tiled=True)
    selected = columns
    gradient = (
        lax.dot_general(
            selected,
            lax.all_gather(key_value_grad, "fsdp", axis=0, tiled=True),
            (((0,), (0,)), ((), ())),
            preferred_element_type=jnp.float32,
        )
        * factor
    )
    selected = columns
    projected = lax.psum_scatter(
        jnp.dot(selected, debiased, preferred_element_type=jnp.float32) * factor,
        "fsdp",
        scatter_dimension=0,
        tiled=True,
    )
    projected = projected.astype(jnp.bfloat16)
    stepped = stored.astype(jnp.float32) - gradient
    moved, moved_weight = along_loop(push_updated, (stepped, weight_sum), round_number)
    renewed = 0.5 * (stepped + moved)
    new_weight = 0.5 * (weight_sum + moved_weight)
    return (projected, renewed.astype(jnp.bfloat16)[None], new_weight)


def solution(mesh):
    placed = (
        P(("site", "fsdp"), None),
        P(),
        P("site", "fsdp", None),
        P("site"),
        P(("site", "fsdp"), None),
        P(),
    )
    return jax.shard_map(
        body,
        mesh=mesh,
        in_specs=placed,
        out_specs=(P(("site", "fsdp"), None), P("site", "fsdp", None), P("site")),
        check_vma=False,
    )
```

profile of v0, /device:TPU:0, one launch (start us, length us, event | category | flops | bytes accessed | tf_op | source)
XLA Modules:
  0.0 305.0 jit_solution(9380837913170041471)
XLA Ops:
  7.2 0.0 copy-start.1
  7.2 1.8 copy.9
  9.0 0.7 fusion.6
  9.7 3.4 %fusion.8 = bf16[128,5120]{0,1:T(8,128)(2,1)} fusion(bf16[128,5120]{0,1:T(8,128)(2,1)S(1)} %copy.9, f32[5120]{0:T(1024)} %param.11, f32[128]{0:T(128)S(1)} %add_rsqrt_fusion), kind=kLoop, calls=%fused_computation.12 | loop fusion | flops 2621440 | bytes 2642432 | tf_op jit(solution)/shard_map/convert_element_type | solution.py:20
  13.1 4.2 %all-to-all-start = ((bf16[128,2,2560]{0,2,1:T(8,128)(2,1)}), bf16[128,2,2560]{0,2,1:T(8,128)(2,1)S(1)}, u32[]{:S(2)}, u32[]{:S(2)}) async-start(bf16[128,2,2560]{0,2,1:T(8,128)(2,1)} %bitcast), calls=%async_computation | async-start | bytes 2621440 | tf_op jit(solution)/shard_map/all_to_all | solution.py:38
  17.3 0.0 reduce-scatter.2.cloned.1.call-start
  18.6 0.0 copy-done.1
  18.7 21.6 %all_gather.3 = bf16[256,1024]{1,0:T(8,128)(2,1)S(1)} all-gather(bf16[128,1024]{1,0:T(8,128)(2,1)S(1)} %copy-done.1), channel_id=1, replica_groups=mesh['site'=16,'fsdp'=2] {'fsdp'}, dimensions={0}, use_global_device_ids=true | all-gather | bytes 786432 | tf_op jit(solution)/shard_map/all_gather | solution.py:43
  40.2 0.0 all-to-all-done
  40.2 0.6 copy.10
  40.9 5.0 %fusion.9 = f32[256,1024]{1,0:T(8,128)} fusion(bf16[256,2560]{1,0:T(8,128)(2,1)S(1)} %bitcast.23, bf16[1,2560,1024]{2,1,0:T(8,128)(2,1)} %param.12, f32[]{:T(128)} %bitcast.19), kind=kOutput, calls=%fused_computation.13 | convolution fusion | flops 1350303744 | bytes 7602180 | tf_op jit(solution)/shard_map/dot_general | solution.py:51
  45.9 0.0 reduce-scatter.2.cloned.1.call-update
  45.9 4.0 %fusion.1 = f32[2560,1024]{1,0:T(8,128)S(1)} fusion(bf16[1,2560,1024]{2,1,0:T(8,128)(2,1)} %param.12, bf16[256,2560]{1,0:T(8,128)(2,1)S(1)} %bitcast.24, bf16[256,1024]{1,0:T(8,128)(2,1)S(1)} %all_gather.3), kind=kOutput, calls=%fused_computation.3 | convolution fusion | flops 1350041600 | bytes 17563648 | tf_op jit(solution)/shard_map/dot_general | solution.py:41
  49.9 0.0 copy-start
  50.0 4.0 %copy-done = f32[2560,1024]{1,0:T(8,128)} copy-done((f32[2560,1024]{1,0:T(8,128)}, f32[2560,1024]{1,0:T(8,128)S(1)}, u32[]{:S(2)}) %copy-start) | copy-done | bytes 10485784
  53.9 228.6 %conditional.1 = (f32[2560,1024]{1,0:T(8,128)}, f32[1]{0:T(128)}) conditional(s32[]{:T(128)} %clamp.3, (f32[2560,1024]{1,0:T(8,128)S(1)}, f32[1]{0:T(128)}) %tuple.24, (f32[2560,1024]{1,0:T(8,128)S(1)}, f32[1]{0:T(128)}) %tuple.24, (f32[2560,1024]{1,0:T(8,128)S(1)}, f32[1]{0:T(128)}) %tuple.24, ...), branch_computations={%region_2.3_spmd, %region_3.4_spmd, %region_4.5_spmd, %region_5.6_... | conditional | bytes 41943152 | solution.py:30
  53.9 1.8 collective-permute-start.4
  55.7 1.6 collective-permute-start.5
  57.3 225.2 %collective-permute-done.5 = f32[1]{0:T(128)} collective-permute-done((f32[1]{0:T(128)}, f32[1]{0:T(128)}, u32[]{:S(2)}, u32[]{:S(2)}) %collective-permute-start.5) | collective-permute-done | bytes 36 | tf_op jit(solution)/shard_map/cond/branch_2_fun/ppermute | solution.py:14
  282.5 0.0 collective-permute-done.4
  283.1 12.2 %fusion.2 = bf16[1,2560,1024]{2,1,0:T(8,128)(2,1)} fusion(f32[2560,1024]{1,0:T(8,128)} %copy-done, f32[2560,1024]{1,0:T(8,128)} %get-tuple-element.29), kind=kLoop, calls=%fused_computation.5 | loop fusion | flops 7864320 | bytes 26214400 | tf_op jit(solution)/shard_map/broadcast_in_dim | solution.py:61
  295.3 0.0 reduce-scatter.2.cloned.1.call-done
  295.3 1.8 convert_element_type.33
  (1 shorter events, 0.0 us)
Async XLA Ops:
  7.2 11.5 %copy-start.1 = (bf16[128,1024]{1,0:T(8,128)(2,1)S(1)}, bf16[128,1024]{1,0:T(8,128)(2,1)}, u32[]{:S(2)}) copy-start(bf16[128,1024]{1,0:T(8,128)(2,1)} %param.14) | copy-start | bytes 786436
  13.1 27.1 %all-to-all-start = ((bf16[128,2,2560]{0,2,1:T(8,128)(2,1)}), bf16[128,2,2560]{0,2,1:T(8,128)(2,1)S(1)}, u32[]{:S(2)}, u32[]{:S(2)}) async-start(bf16[128,2,2560]{0,2,1:T(8,128)(2,1)} %bitcast), calls=%async_computation | async-start | bytes 2621440 | tf_op jit(solution)/shard_map/all_to_all | solution.py:38
  17.3 278.0 %reduce-scatter.2.cloned.1.call-start = ((), (), s32[]{:S(2)}) async-start(), calls=%async_computation.2 | async-start | bytes 1572864 | tf_op jit(solution)/shard_map/reduce_scatter | solution.py:50
  49.9 4.0 %copy-start = (f32[2560,1024]{1,0:T(8,128)}, f32[2560,1024]{1,0:T(8,128)S(1)}, u32[]{:S(2)}) copy-start(f32[2560,1024]{1,0:T(8,128)S(1)} %fusion.1) | copy-start | bytes 31457284
  53.9 228.6 %collective-permute-start.4 = (f32[2560,1024]{1,0:T(8,128)S(1)}, f32[2560,1024]{1,0:T(8,128)}, u32[]{:S(2)}, u32[]{:S(2)}) collective-permute-start(f32[2560,1024]{1,0:T(8,128)S(1)} %get-tuple-element.20), channel_id=1, source_target_pairs={{24,0},{26,2},{28,4},{30,6},{0,8},{2,10},{4,12},{6,14},{8,16},{10,... | collective-permute-start | bytes 31457288 | tf_op jit(solution)/shard_map/cond/branch_2_fun/ppermute | solution.py:14
  55.7 226.7 %collective-permute-start.5 = (f32[1]{0:T(128)}, f32[1]{0:T(128)}, u32[]{:S(2)}, u32[]{:S(2)}) collective-permute-start(f32[1]{0:T(128)} %get-tuple-element.21), channel_id=1, source_target_pairs={{24,0},{26,2},{28,4},{30,6},{0,8},{2,10},{4,12},{6,14},{8,16},{10,... | collective-permute-start | bytes 20 | tf_op jit(solution)/shard_map/cond/branch_2_fun/ppermute | solution.py:14
Sparse Core Ops, SparseCore 0:
  46.0 20.8 reduce-scatter.1
where the time goes:
time: 305 us
  waiting for transfers between devices  225 us (74%)
  blocking collectives  21.6 us (7%)
  other arithmetic  18.1 us (6%)
  between operations  17.1 us (6%)
  matrix products  9.06 us (3%)
  starting transfers between devices  7.61 us (2%)
  local copies, waits for them, and re-layouts  6.4 us (2%)
    ppermute x2, waiting for transfers between devices, shifted(): return lax.ppermute(block, axis, route)  225 us
    all_gather x1, blocking collectives, body(): lax.all_gather(key_value_grad, 'fsdp', axis=0, tiled=True)  21.6 us
    broadcast_in_dim x1, other arithmetic, body(): return (projected, renewed.astype(jnp.bfloat16)[None], new_weight)  12.2 us
  transfers between devices with their start and end apart: 4, of which 1 were waited for; matrix products, arithmetic and copies ran while one was open for 5% of the time, Pallas kernels for 0%

commit v1 on v0

v1 whole, which is shorter than its diff:
```python
from functools import partial

import jax
import jax.numpy as jnp
from jax import lax
from jax.experimental import pallas as pl
from jax.experimental.pallas import tpu as pltpu
from jax.sharding import PartitionSpec as P

KMAX = 4
C = 128
F32, BF16 = jnp.float32, jnp.bfloat16


def kernel(
    offset, sites, shards, factor,
    tokens, gain, state, weight, grads,
    projected, renewed, new_weight,
    tok, gall, cols, nsend, inv, held, own, push, landed, out, acc, terms, outp, wsend, wland,
    load_sem, gsend_sem, grecv_sem, csend_sem, crecv_sem, st_sem, psend_sem, precv_sem,
    out_sem, tsend_sem, trecv_sem, w_sem, outp_sem,
):
    chunks, _, width = held.shape
    rows, features = tok.shape
    block = chunks * C
    me = lax.axis_index("fsdp")
    site = lax.axis_index("site")
    ahead = lax.rem(site + offset, sites)
    behind = lax.rem(site + (sites - offset), sites)
    mine = pl.ds(pl.multiple_of(me * rows, rows), rows)

    def peer(j):
        return lax.rem(me + j, shards)

    def remote(src, dst, send, recv, device):
        return pltpu.make_async_remote_copy(
            src_ref=src, dst_ref=dst, send_sem=send, recv_sem=recv,
            device_id=device, device_id_type=pl.DeviceIdType.MESH,
        )

    def grad_copy(j):
        return remote(grads, gall.at[mine], gsend_sem.at[j - 1], grecv_sem.at[j - 1], {"fsdp": peer(j)})

    def cols_copy(j, c):
        return remote(
            nsend.at[j - 1, c], cols.at[c, mine], csend_sem.at[j - 1, c], crecv_sem.at[j - 1, c],
            {"fsdp": peer(j)},
        )

    def push_copy(c):
        return remote(push.at[c], landed.at[c], psend_sem.at[c], precv_sem.at[c], {"site": ahead})

    def terms_copy(j):
        theirs = pl.ds(pl.multiple_of(peer(j) * rows, rows), rows)
        return remote(
            acc.at[theirs], terms.at[j - 1], tsend_sem.at[j - 1], trecv_sem.at[j - 1], {"fsdp": peer(j)}
        )

    def weight_copy():
        return remote(wsend, wland, w_sem.at[0], w_sem.at[1], {"site": ahead})

    def chunk_rows(c):
        return pl.ds(pl.multiple_of(c * C, C), C)

    def held_copy(c):
        return pltpu.make_async_copy(state.at[0, chunk_rows(c)], held.at[c], st_sem.at[c])

    def out_copy(c):
        return pltpu.make_async_copy(out.at[c], renewed.at[0, chunk_rows(c)], out_sem.at[c])

    tok_load = pltpu.make_async_copy(tokens, tok, load_sem.at[0])
    grad_load = pltpu.make_async_copy(grads, gall.at[mine], load_sem.at[1])
    tok_load.start()
    grad_load.start()

    barrier = pltpu.get_barrier_semaphore()
    for j in range(1, shards):
        pl.semaphore_signal(
            barrier, inc=1, device_id={"fsdp": peer(j)}, device_id_type=pl.DeviceIdType.MESH
        )
    for other in (ahead, behind):
        pl.semaphore_signal(
            barrier, inc=1, device_id={"site": other}, device_id_type=pl.DeviceIdType.MESH
        )
    pl.semaphore_wait(barrier, shards + 1)

    for j in range(1, shards):
        grad_copy(j).start()

    @pl.loop(0, chunks)
    def _(c):
        held_copy(c).start()

    w = weight[0]
    wsend[...] = jnp.full(wsend.shape, w, F32)
    weight_copy().start()

    tok_load.wait()

    def squares(i, total):
        v = tok[:, pl.ds(pl.multiple_of(i * 128, 128), 128)].astype(F32)
        return total + v * v

    total = lax.fori_loop(0, features // 128, squares, jnp.zeros((rows, 128), F32))
    mean = jnp.sum(total, axis=1, keepdims=True) * (1.0 / features)
    inv[...] = jnp.broadcast_to(lax.rsqrt(mean + 1e-06), inv.shape)

    def piece(p, c):
        at = pl.ds(pl.multiple_of(p * block + c * C, C), C)
        return (tok[:, at].astype(F32) * inv[...] * gain[:, at]).astype(BF16)

    @pl.loop(0, chunks)
    def _(c):
        for j in range(1, shards):
            nsend[j - 1, c] = piece(peer(j), c)
            cols_copy(j, c).start()

    @pl.loop(0, chunks)
    def _(c):
        cols[c, mine] = piece(me, c)

    grad_load.wait()
    for j in range(1, shards):
        grad_copy(j).wait_recv()

    @pl.loop(0, chunks)
    def _(c):
        held_copy(c).wait()
        for j in range(1, shards):
            cols_copy(j, c).wait_recv()
        gradient = lax.dot_general(
            cols[c], gall[...], (((0,), (0,)), ((), ())), preferred_element_type=F32
        )
        stepped = held[c].astype(F32) - gradient * factor
        own[c] = stepped
        push[c] = stepped.astype(BF16)
        push_copy(c).start()

    acc[...] = jnp.zeros_like(acc)

    @pl.loop(0, chunks)
    def _(c):
        debiased = (held[c].astype(F32) / w).astype(BF16)
        acc[...] += jnp.dot(cols[c], debiased, preferred_element_type=F32)

    for j in range(1, shards):
        terms_copy(j).start()
    for j in range(1, shards):
        terms_copy(j).wait_recv()
    total = acc[mine]
    for j in range(1, shards):
        total = total + terms[j - 1]
    outp[...] = (total * factor).astype(BF16)
    outp_copy = pltpu.make_async_copy(outp, projected, outp_sem.at[0])
    outp_copy.start()

    @pl.loop(0, chunks)
    def _(c):
        push_copy(c).wait_recv()
        out[c] = (0.5 * (own[c] + landed[c].astype(F32))).astype(BF16)
        out_copy(c).start()

    weight_copy().wait()
    new_weight[0] = 0.5 * (w + jnp.max(wland[...]))

    for j in range(1, shards):
        grad_copy(j).wait_send()
        terms_copy(j).wait_send()
    outp_copy.wait()

    @pl.loop(0, chunks)
    def _(c):
        for j in range(1, shards):
            cols_copy(j, c).wait_send()
        push_copy(c).wait_send()
        out_copy(c).wait()


def round_with(offset_index, sites, shards, tokens, norm_gain, state, weight_sum, grads):
    rows, features = tokens.shape
    _, block, width = state.shape
    chunks = block // C
    others = max(shards - 1, 1)
    dma = pltpu.SemaphoreType.DMA
    anywhere = pl.BlockSpec(memory_space=pl.ANY)
    vmem = pl.BlockSpec(memory_space=pltpu.VMEM)
    smem = pl.BlockSpec(memory_space=pltpu.SMEM)
    return pl.pallas_call(
        partial(kernel, 2**offset_index, sites, shards, features ** (-0.5)),
        out_shape=(
            jax.ShapeDtypeStruct((rows, width), BF16),
            jax.ShapeDtypeStruct(state.shape, BF16),
            jax.ShapeDtypeStruct((1,), F32),
        ),
        in_specs=[anywhere, vmem, anywhere, smem, anywhere],
        out_specs=(anywhere, anywhere, smem),
        scratch_shapes=[
            pltpu.VMEM((rows, features), BF16),
            pltpu.VMEM((shards * rows, width), BF16),
            pltpu.VMEM((chunks, shards * rows, C), BF16),
            pltpu.VMEM((others, chunks, rows, C), BF16),
            pltpu.VMEM((rows, C), F32),
            pltpu.VMEM((chunks, C, width), BF16),
            pltpu.VMEM((chunks, C, width), F32),
            pltpu.VMEM((chunks, C, width), BF16),
            pltpu.VMEM((chunks, C, width), BF16),
            pltpu.VMEM((chunks, C, width), BF16),
            pltpu.VMEM((shards * rows, width), F32),
            pltpu.VMEM((others, rows, width), F32),
            pltpu.VMEM((rows, width), BF16),
            pltpu.VMEM((8, 128), F32),
            pltpu.VMEM((8, 128), F32),
            dma((2,)),
            dma((others,)),
            dma((others,)),
            dma((others, chunks)),
            dma((others, chunks)),
            dma((chunks,)),
            dma((chunks,)),
            dma((chunks,)),
            dma((chunks,)),
            dma((others,)),
            dma((others,)),
            dma((2,)),
            dma((1,)),
        ],
        compiler_params=pltpu.CompilerParams(
            collective_id=offset_index, has_side_effects=True, vmem_limit_bytes=56 * 2**20
        ),
        name=f"round_{offset_index}",
    )(tokens, norm_gain, state, weight_sum, grads)


def solution(mesh):
    sites, shards = mesh.shape["site"], mesh.shape["fsdp"]

    def body(tokens, norm_gain, state, weight_sum, key_value_grad, round_number):
        branches = [partial(round_with, k, sites, shards) for k in range(KMAX)]
        which = jnp.remainder(round_number[0], jnp.int32(KMAX))
        return lax.switch(
            which, branches, tokens, norm_gain.reshape(1, -1), state, weight_sum, key_value_grad
        )

    tokens_spec = P(("site", "fsdp"), None)
    state_spec = P("site", "fsdp", None)
    return jax.shard_map(
        body,
        mesh=mesh,
        in_specs=(tokens_spec, P(), state_spec, P("site"), tokens_spec, P()),
        out_specs=(tokens_spec, state_spec, P("site")),
        check_vma=False,
    )
```

time: 305 us -> 251 us (0.82)
  Pallas kernels: 0 us -> 242 us
  waiting for transfers between devices: 225 us -> 0 us
  blocking collectives: 21.6 us -> 0 us
  other arithmetic: 18.1 us -> 0 us
  between operations: 17.1 us -> 3 us
  matrix products: 9.06 us -> 0 us
  starting transfers between devices: 7.61 us -> 0 us
    pallas_call x0 -> x1, Pallas kernels: none -> 242 us  [round_with(): pl.pallas_call(partial(kernel, 2 ** offset_index, sites, shards, features...]
    ppermute x2 -> x0, waiting for transfers between devices: 225 us -> none  [shifted(): return lax.ppermute(block, axis, route)]
    all_gather x1 -> x0, blocking collectives: 21.6 us -> none  [body(): lax.all_gather(key_value_grad, 'fsdp', axis=0, tiled=True)]
    broadcast_in_dim x1 -> x0, other arithmetic: 12.2 us -> none  [body(): return (projected, renewed.astype(jnp.bfloat16)[None], new_weight)]
    dot_general x2 -> x0, matrix products: 9.06 us -> none  [the longest x1 5.01 us: body(): jnp.dot(selected, debiased, preferred_element_type=jnp.float32) * factor]
    convert_element_type x2 -> x0, other arithmetic: 5.18 us -> none  [the longest x1 3.41 us: rms_normed(): return (values * inverse * norm_gain).astype(jnp.bfloat16)]
    all_to_all x1 -> x0, starting transfers between devices: 4.23 us -> none  [body(): lax.all_to_all(normed, 'fsdp', split_axis=1, concat_axis=0, tiled=True)]
    ppermute x2 -> x0, starting transfers between devices: 3.37 us -> none  [shifted(): return lax.ppermute(block, axis, route)]
  transfers between devices with their start and end apart: 4 -> 0, of which waited for: 1 -> 0; matrix products, arithmetic and copies ran while one was open for 5% -> 0% of each run, Pallas kernels for 0% -> 0%
where the time goes in v1:
time: 251 us
  Pallas kernels  242 us (96%)
  local copies, waits for them, and re-layouts  6.12 us (2%)
  between operations  3 us (1%)
    pallas_call x1, Pallas kernels, round_with(): pl.pallas_call(partial(kernel, 2 ** offset_index, sites, shards, features...  242 us
    unnamed x2, local copies, waits for them, and re-layouts  6.12 us

profile of v1, /device:TPU:0, one launch (start us, length us, event | category | flops | bytes accessed | tf_op | source)
XLA Modules:
  0.0 250.8 jit_solution(1309460354257486990)
XLA Ops:
  1.3 241.6 %conditional.1 = ((bf16[128,1024]{1,0:T(8,128)(2,1)S(1)}, bf16[1,2560,1024]{2,1,0:T(8,128)(2,1)}, f32[1]{0:T(128)})) conditional(s32[]{:T(128)} %clamp.3, (bf16[128,5120]{1,0:T(8,128)(2,1)}, f32[1,5120]{1,0:T(1,128)}, bf16[1,2560,1024]{2,1,0:T(8,128)(2,1)}, f32[1]{0:T(128)}, bf16[128,1024]{1,0:T(8,128)(2,1)}) %tuple.42, ...), branch_computations={%region_0.1_spmd, %region_1.2_spmd, %region_2.3_spmd, %region_3.4_... | conditional | bytes 8 | solution.py:240
  1.3 241.6 %round_3.1 = (bf16[128,1024]{1,0:T(8,128)(2,1)S(1)}, bf16[1,2560,1024]{2,1,0:T(8,128)(2,1)}, f32[1]{0:T(128)}) custom-call(bf16[128,5120]{1,0:T(8,128)(2,1)} %get-tuple-element.55.tokens, f32[1,5120]{1,0:T(1,128)} %get-tuple-element.56.gain, bf16[1,2560,1024]{2,1,0:T(8,128)(2,1)} %get-tuple-element.57.state, f32[1]{0:T(128)} %get-tuple-element.58.weight, ...), custom_call_target="tpu_custom_call" | custom-call | tf_op jit(solution)/shard_map/cond/branch_3_fun/round_3/pallas_call | solution.py:188
  242.9 0.7 copy.37
  243.6 5.4 %copy.38 = bf16[1,2560,1024]{2,1,0:T(8,128)(2,1)} copy(bf16[1,2560,1024]{2,1,0:T(8,128)(2,1)} %get-tuple-element.94) | data formatting | bytes 10485760

commit v2 on v1

v2 whole, which is shorter than its diff:
```python
from functools import partial

import jax
import jax.numpy as jnp
from jax import lax
from jax.experimental import pallas as pl
from jax.experimental.pallas import tpu as pltpu
from jax.sharding import PartitionSpec as P

KMAX = 4
GROUPS = 4
LEAD = 2
F32, BF16 = jnp.float32, jnp.bfloat16


def kernel(
    offset, sites, shards, factor,
    tokens, gain, state, weight, grads,
    projected, renewed, new_weight,
    tok, gall, cols, nsend, inv, held, own, push, landed, acc, terms, wsend, wland,
    load_sem, gsend_sem, grecv_sem, csend_sem, crecv_sem, st_sem, psend_sem, precv_sem,
    tsend_sem, trecv_sem, w_sem,
):
    chunks, C, width = held.shape
    rows, features = tok.shape
    block = chunks * C
    part = width // GROUPS
    me = lax.axis_index("fsdp")
    site = lax.axis_index("site")
    ahead = lax.rem(site + offset, sites)
    behind = lax.rem(site + (sites - offset), sites)
    mine = pl.ds(pl.multiple_of(me * rows, rows), rows)

    def peer(j):
        return lax.rem(me + j, shards)

    def remote(src, dst, send, recv, device):
        return pltpu.make_async_remote_copy(
            src_ref=src, dst_ref=dst, send_sem=send, recv_sem=recv,
            device_id=device, device_id_type=pl.DeviceIdType.MESH,
        )

    def group(q):
        return pl.ds(pl.multiple_of(q * part, part), part)

    def grad_copy(j, q):
        return remote(
            grads.at[:, group(q)], gall.at[q, mine], gsend_sem.at[j - 1, q], grecv_sem.at[j - 1, q],
            {"fsdp": peer(j)},
        )

    def grad_load(q):
        return pltpu.make_async_copy(grads.at[:, group(q)], gall.at[q, mine], load_sem.at[1 + q])

    def cols_copy(j, c):
        return remote(
            nsend.at[j - 1, c], cols.at[c, mine], csend_sem.at[j - 1, c], crecv_sem.at[j - 1, c],
            {"fsdp": peer(j)},
        )

    def push_copy(u):
        return remote(push.at[u], landed.at[u], psend_sem.at[u], precv_sem.at[u], {"site": ahead})

    def terms_copy(j):
        theirs = pl.ds(pl.multiple_of(peer(j) * rows, rows), rows)
        return remote(
            acc.at[theirs], terms.at[j - 1], tsend_sem.at[j - 1], trecv_sem.at[j - 1], {"fsdp": peer(j)}
        )

    def weight_copy():
        return remote(wsend, wland, w_sem.at[0], w_sem.at[1], {"site": ahead})

    def chunk_rows(c):
        return pl.ds(pl.multiple_of(c * C, C), C)

    def held_copy(c):
        return pltpu.make_async_copy(state.at[0, chunk_rows(c)], held.at[c], st_sem.at[c])

    tok_load = pltpu.make_async_copy(tokens, tok, load_sem.at[0])
    tok_load.start()
    for q in range(GROUPS):
        grad_load(q).start()

    barrier = pltpu.get_barrier_semaphore()
    for j in range(1, shards):
        pl.semaphore_signal(
            barrier, inc=1, device_id={"fsdp": peer(j)}, device_id_type=pl.DeviceIdType.MESH
        )
    for other in (ahead, behind):
        pl.semaphore_signal(
            barrier, inc=1, device_id={"site": other}, device_id_type=pl.DeviceIdType.MESH
        )

    @pl.loop(0, chunks)
    def _(c):
        held_copy(c).start()

    w = weight[0]
    wsend[...] = jnp.full(wsend.shape, w, F32)
    tok_load.wait()

    def squares(i, total):
        v = tok[:, pl.ds(pl.multiple_of(i * 128, 128), 128)].astype(F32)
        return total + v * v

    total = lax.fori_loop(0, features // 128, squares, jnp.zeros((rows, 128), F32), unroll=4)
    mean = jnp.sum(total, axis=1, keepdims=True) * (1.0 / features)
    inv[...] = jnp.broadcast_to(lax.rsqrt(mean + 1e-06), inv.shape)

    def piece(p, c):
        at = pl.ds(pl.multiple_of(p * block + c * C, C), C)
        return (tok[:, at].astype(F32) * inv[...] * gain[:, at]).astype(BF16)

    def send_pieces(c):
        for j in range(1, shards):
            nsend[j - 1, c] = piece(peer(j), c)
            cols_copy(j, c).start()

    def send_grads(q):
        for j in range(1, shards):
            grad_copy(j, q).start()

    for j in range(1, shards):
        nsend[j - 1, 0] = piece(peer(j), 0)
    pl.semaphore_wait(barrier, shards + 1)
    send_grads(0)
    for j in range(1, shards):
        cols_copy(j, 0).start()
    for q in range(1, LEAD + 1):
        send_grads(q)

    def step(q, c):
        u = c * GROUPS + q
        gradient = lax.dot_general(
            cols[c], gall[q], (((0,), (0,)), ((), ())), preferred_element_type=F32
        )
        stepped = held[c, :, group(q)].astype(F32) - gradient * factor
        own[u] = stepped
        push[u] = stepped.astype(BF16)
        push_copy(u).start()

    def grads_here(q):
        grad_load(q).wait()
        for j in range(1, shards):
            grad_copy(j, q).wait_recv()

    cols[0, mine] = piece(me, 0)
    held_copy(0).wait()
    for j in range(1, shards):
        cols_copy(j, 0).wait_recv()
    for q in range(GROUPS):
        grads_here(q)
        step(q, 0)
        if q + LEAD + 1 < GROUPS:
            send_grads(q + LEAD + 1)
        elif q + LEAD + 1 - GROUPS < LEAD:
            send_pieces(q + LEAD + 2 - GROUPS)
    weight_copy().start()

    @pl.loop(1, chunks)
    def _(c):
        @pl.when(c + LEAD < chunks)
        def _():
            send_pieces(c + LEAD)

        cols[c, mine] = piece(me, c)
        held_copy(c).wait()
        for j in range(1, shards):
            cols_copy(j, c).wait_recv()
        for q in range(GROUPS):
            step(q, c)

    acc[...] = jnp.zeros_like(acc)

    @pl.loop(0, chunks)
    def _(c):
        debiased = (held[c].astype(F32) / w).astype(BF16)
        acc[...] += jnp.dot(cols[c], debiased, preferred_element_type=F32)

    for j in range(1, shards):
        terms_copy(j).start()
    for j in range(1, shards):
        terms_copy(j).wait_recv()
    total = acc[mine]
    for j in range(1, shards):
        total = total + terms[j - 1]
    projected[...] = (total * factor).astype(BF16)

    @pl.loop(0, chunks)
    def _(c):
        for q in range(GROUPS):
            u = c * GROUPS + q
            push_copy(u).wait_recv()
            mixed = 0.5 * (own[u] + landed[u].astype(F32))
            renewed[0, chunk_rows(c), group(q)] = mixed.astype(BF16)

    weight_copy().wait()
    new_weight[0] = 0.5 * (w + jnp.max(wland[...]))

    for j in range(1, shards):
        terms_copy(j).wait_send()
        for q in range(GROUPS):
            grad_copy(j, q).wait_send()

    @pl.loop(0, chunks)
    def _(c):
        for j in range(1, shards):
            cols_copy(j, c).wait_send()

    @pl.loop(0, GROUPS * chunks)
    def _(u):
        push_copy(u).wait_send()


def store(projected, renewed, projected_out, renewed_out, sem):
    copies = [
        pltpu.make_async_copy(renewed, renewed_out, sem.at[0]),
        pltpu.make_async_copy(projected, projected_out, sem.at[1]),
    ]
    for copy in copies:
        copy.start()
    for copy in copies:
        copy.wait()


def round_with(offset_index, sites, shards, tokens, norm_gain, state, weight_sum, grads):
    rows, features = tokens.shape
    _, block, width = state.shape
    C = 256 if block % 256 == 0 else 128
    chunks, part = block // C, width // GROUPS
    others = max(shards - 1, 1)
    dma = pltpu.SemaphoreType.DMA
    anywhere = pl.BlockSpec(memory_space=pl.ANY)
    vmem = pl.BlockSpec(memory_space=pltpu.VMEM)
    smem = pl.BlockSpec(memory_space=pltpu.SMEM)
    projected, renewed, new_weight = pl.pallas_call(
        partial(kernel, 2**offset_index, sites, shards, features ** (-0.5)),
        out_shape=(
            pltpu.VMEM((rows, width), BF16),
            pltpu.VMEM(state.shape, BF16),
            jax.ShapeDtypeStruct((1,), F32),
        ),
        in_specs=[anywhere, vmem, anywhere, smem, anywhere],
        out_specs=(vmem, vmem, smem),
        scratch_shapes=[
            pltpu.VMEM((rows, features), BF16),
            pltpu.VMEM((GROUPS, shards * rows, part), BF16),
            pltpu.VMEM((chunks, shards * rows, C), BF16),
            pltpu.VMEM((others, chunks, rows, C), BF16),
            pltpu.VMEM((rows, C), F32),
            pltpu.VMEM((chunks, C, width), BF16),
            pltpu.VMEM((GROUPS * chunks, C, part), F32),
            pltpu.VMEM((GROUPS * chunks, C, part), BF16),
            pltpu.VMEM((GROUPS * chunks, C, part), BF16),
            pltpu.VMEM((shards * rows, width), F32),
            pltpu.VMEM((others, rows, width), F32),
            pltpu.VMEM((8, 128), F32),
            pltpu.VMEM((8, 128), F32),
            dma((1 + GROUPS,)),
            dma((others, GROUPS)),
            dma((others, GROUPS)),
            dma((others, chunks)),
            dma((others, chunks)),
            dma((chunks,)),
            dma((GROUPS * chunks,)),
            dma((GROUPS * chunks,)),
            dma((others,)),
            dma((others,)),
            dma((2,)),
        ],
        compiler_params=pltpu.CompilerParams(
            collective_id=offset_index, has_side_effects=True, vmem_limit_bytes=48 * 2**20
        ),
        name=f"round_{offset_index}",
    )(tokens, norm_gain, state, weight_sum, grads)
    projected, renewed = pl.pallas_call(
        store,
        out_shape=(
            jax.ShapeDtypeStruct((rows, width), BF16),
            jax.ShapeDtypeStruct(state.shape, BF16),
        ),
        in_specs=[anywhere, anywhere],
        out_specs=(anywhere, anywhere),
        scratch_shapes=[dma((2,))],
        compiler_params=pltpu.CompilerParams(vmem_limit_bytes=2**20),
        name=f"store_{offset_index}",
    )(projected, renewed)
    return projected, renewed, new_weight


def solution(mesh):
    sites, shards = mesh.shape["site"], mesh.shape["fsdp"]

    def body(tokens, norm_gain, state, weight_sum, key_value_grad, round_number):
        branches = [partial(round_with, k, sites, shards) for k in range(KMAX)]
        which = jnp.remainder(round_number[0], jnp.int32(KMAX))
        return lax.switch(
            which, branches, tokens, norm_gain.reshape(1, -1), state, weight_sum, key_value_grad
        )

    tokens_spec = P(("site", "fsdp"), None)
    state_spec = P("site", "fsdp", None)
    return jax.shard_map(
        body,
        mesh=mesh,
        in_specs=(tokens_spec, P(), state_spec, P("site"), tokens_spec, P()),
        out_specs=(tokens_spec, state_spec, P("site")),
        check_vma=False,
    )
```

time: 251 us -> 78.9 us (0.31)
  Pallas kernels: 242 us -> 75.6 us
  local copies, waits for them, and re-layouts: 6.12 us -> 0 us
    pallas_call x1, Pallas kernels: 242 us -> 73.1 us  [round_with(): pl.pallas_call(partial(kernel, 2 ** offset_index, sites, shards, features...]
    unnamed x2 -> x0, local copies, waits for them, and re-layouts: 6.12 us -> none
where the time goes in v2:
time: 78.9 us; the launch traced here: 78.7 us
  Pallas kernels  75.6 us (96%)
  between operations  3.06 us (4%)
    pallas_call x1, Pallas kernels, round_with(): pl.pallas_call(partial(kernel, 2 ** offset_index, sites, shards, features...  73.1 us
    pallas_call x1, Pallas kernels, round_with(): pl.pallas_call(store, out_shape=(jax.ShapeDtypeStruct((rows, width), BF16...  2.45 us

profile of v2, /device:TPU:0, one launch (start us, length us, event | category | flops | bytes accessed | tf_op | source)
XLA Modules:
  0.0 78.7 jit_solution(16822359482309050311)
XLA Ops:
  1.3 75.6 %conditional.1 = (bf16[128,1024]{1,0:T(8,128)(2,1)}, bf16[1,2560,1024]{2,1,0:T(8,128)(2,1)}, f32[1]{0:T(128)}) conditional(s32[]{:T(128)} %clamp.3, (bf16[128,5120]{1,0:T(8,128)(2,1)}, f32[1,5120]{1,0:T(1,128)}, bf16[1,2560,1024]{2,1,0:T(8,128)(2,1)}, f32[1]{0:T(128)}, bf16[128,1024]{1,0:T(8,128)(2,1)}) %tuple.30, ...), branch_computations={%region_0.1_spmd, %region_1.2_spmd, %region_2.3_spmd, %region_3.4_... | conditional | bytes 24 | solution.py:297
  1.3 73.1 %round_0.1 = (bf16[128,1024]{1,0:T(8,128)(2,1)S(1)}, bf16[1,2560,1024]{2,1,0:T(8,128)(2,1)S(1)}, f32[1]{0:T(128)}) custom-call(bf16[128,5120]{1,0:T(8,128)(2,1)} %get-tuple-element.40.tokens, f32[1,5120]{1,0:T(1,128)} %get-tuple-element.41.gain, bf16[1,2560,1024]{2,1,0:T(8,128)(2,1)} %get-tuple-element.42.state, f32[1]{0:T(128)} %get-tuple-element.43.weight, ...), custom_call_target="tpu_custom_call" | custom-call | tf_op jit(solution)/shard_map/cond/branch_0_fun/round_0/pallas_call | solution.py:236
  74.5 2.4 %store_0.1 = (bf16[128,1024]{1,0:T(8,128)(2,1)}, bf16[1,2560,1024]{2,1,0:T(8,128)(2,1)}) custom-call(bf16[128,1024]{1,0:T(8,128)(2,1)S(1)} %get-tuple-element.45.projected, bf16[1,2560,1024]{2,1,0:T(8,128)(2,1)S(1)} %get-tuple-element.46.renewed), custom_call_target="tpu_custom_call" | custom-call | tf_op jit(solution)/shard_map/cond/branch_0_fun/store_0/pallas_call | solution.py:276
